TPU v7x, 32 devices: a whole 2x2x4 slice. The times are simulated.
32 devices in a mesh: aa: 8 (over y, x, core), col: 4 (over z).
Axes of the slice: x: 2, y: 2, z: 4, core: 2. Of those that a mesh axis runs over, the one named last changes fastest.
Arguments:
- fit_ac: float32 [512, 512, 2048], P('aa', 'col'), may hold values from -0.125 to 0.125
- fit_bd: float32 [2048, 1024], P(('aa', 'col')), may hold values from -6 to 6
- amplitudes: float32 [2, 32, 512, 256], P(None, 'aa', 'col'), may hold values from -0.046875 to 0.046875
Outputs:
- residual: float32 [2, 16, 512, 256], P(None, 'col', 'aa')
All inputs are finite; a program needn't handle non-finite values.
Results may differ from a plain program's by a relative error of at most 0.0003.
Values sent between devices are 32-bit elements; how exact they have to be, the bound alone decides.
A program may use at most 192 MiB of HBM per device.

v0:
```python
import functools

import jax
import jax.numpy as jnp
from jax import lax
from jax.experimental import pallas as pl
from jax.experimental.pallas import tpu as pltpu
from jax.sharding import PartitionSpec as P

F32 = jnp.float32
BF16 = jnp.bfloat16
F8 = jnp.float8_e4m3fn
NT = (((1,), (1,)), ((), ()))
MESH = pl.DeviceIdType.MESH
VMEM_LIMIT = 67_000_000

A_HI, A_LO, B_HI, B_LO = 2.0**11, 2.0**20, 2.0**5, 2.0**14
SCALE, UNDO = 2.0**25, 2.0**-25
LANES = 128
PARTS = 2


def split(value):
    high = value.astype(BF16)
    return high, value - high.astype(F32)


class Plan:
    def __init__(self, n_aa, n_col, fit_ac, fit_bd, amplitudes):
        self.n_aa, self.n_col = n_aa, n_col
        self.a_local, self.c_local, self.count_q = fit_ac.shape
        self.blocks, self.d_local, _, self.pairs = amplitudes.shape
        self.q_local, self.columns = fit_bd.shape
        self.d_size = self.d_local * n_aa
        self.b_size = self.columns // (self.blocks * self.d_size)
        self.b_out = self.b_size // n_col
        self.near = min(n_col, max(1, LANES // self.q_local))
        self.halves = n_col // self.near
        self.depth = self.near * self.q_local
        self.far = [1 << bit for bit in range(1, n_aa.bit_length() - 1)]
        self.orders = [self.far, self.far[::-1]]
        masks = [mask for mask in range(0, n_aa, 2)]
        ones = [m for m in masks if m.bit_count() == 1]
        more = [m for m in masks if m.bit_count() > 1]
        rest = range(1, self.halves)
        own = [(m, 0) for m in (0,)]
        self.phases = [own, [(m, 0) for m in ones], [(m, 0) for m in more] + [(0, r) for r in rest]]
        self.phases.append([(m, r) for r in rest for m in ones + more])
        self.phases = [[(m ^ core, r) for m, r in phase for core in (0, 1)] for phase in self.phases if phase]
        self.group = min(self.a_local, 16)
        self.rows = [8 if len(phase) <= 4 else 4 for phase in self.phases]
        self.waves = [[], [], []]
        for part, order in enumerate(self.orders):
            for mask in sorted(masks[1:], key=lambda m: m.bit_count()):
                stage = max(order.index(bit) for bit in self.far if bit & mask)
                wave = 2 if mask.bit_count() > 1 else (0 if stage == 0 else 1)
                self.waves[wave].append((part, mask, order[stage], order[stage + 1 :]))
        self.waves[2].sort(key=lambda one: one[1].bit_count())
        self.moves = PARTS * (n_aa // 2 - 1 + n_aa // 2)


class Exchange:
    def __init__(self, plan, source, target, send, recv, place):
        self.plan, self.source, self.target = plan, source, target
        self.send, self.recv, self.place, self.keys = send, recv, place, {}

    def copy(self, part, mask, bit):
        index = self.keys.setdefault((part, mask, bit), len(self.keys))
        aa, col = self.place
        return pltpu.make_async_remote_copy(
            src_ref=self.source(part, mask),
            dst_ref=self.target(part, mask),
            send_sem=self.send.at[index],
            recv_sem=self.recv.at[index],
            device_id=(aa ^ bit, col),
            device_id_type=MESH,
        )

    def own(self):
        for stage in range(len(self.plan.far)):
            for part, order in enumerate(self.plan.orders):
                self.copy(part, 0, order[stage]).start()
        for part in range(PARTS):
            self.copy(part, 0, 1).start()

    def wave(self, which):
        for part, mask, bit, later in self.plan.waves[which]:
            self.copy(part, mask ^ bit, bit).wait_recv()
            for further in later:
                self.copy(part, mask, further).start()
            self.copy(part, mask, 1).start()

    def core(self, mask):
        for part in range(PARTS):
            self.copy(part, mask ^ 1, 1).wait_recv()

    def finish(self):
        for key in list(self.keys):
            self.copy(*key).wait_send()


def kernel(
    plan, fit_ac, fit_bd, amplitudes, sums, bd_all, t_all,
    acc, high, low8, high8, t_high, t_low, blocks_a, stage, turned, t_stage, made, ready,
    a_sem, own_sem, stage_sem, t_sem, z_send, z_recv, x_send, x_recv, r_send, r_recv, r_own,
):
    aa, col = lax.axis_index("aa").astype(jnp.int32), lax.axis_index("col").astype(jnp.int32)
    n_col, n_aa = plan.n_col, plan.n_aa
    q_local, depth, d_local = plan.q_local, plan.depth, plan.d_local
    half = plan.columns // PARTS

    barrier = pltpu.get_barrier_semaphore()
    peers = [(aa, col ^ step) for step in range(1, n_col)] + [(aa ^ bit, col) for bit in [1] + plan.far]
    for peer in peers:
        pl.semaphore_signal(barrier, inc=1, device_id=peer, device_id_type=MESH)

    mine = pl.ds(pl.multiple_of((aa * n_col + col) * q_local, q_local), q_local)
    take = pltpu.make_async_copy(fit_bd, stage.at[0, pl.ds(0, q_local)], own_sem.at[0])
    take.start()
    keep = pltpu.make_async_copy(amplitudes, t_all.at[:, pl.ds(aa * d_local, d_local)], own_sem.at[1])
    keep.start()
    pl.semaphore_wait(barrier, len(peers))

    along = []
    for step in range(1, n_col):
        along.append(
            pltpu.make_async_remote_copy(
                src_ref=fit_bd,
                dst_ref=bd_all.at[mine],
                send_sem=z_send.at[step - 1],
                recv_sem=z_recv.at[step - 1],
                device_id=(aa, col ^ step),
                device_id_type=MESH,
            )
        )
        along[-1].start()
    take.wait()
    put = pltpu.make_async_copy(stage.at[0, pl.ds(0, q_local)], bd_all.at[mine], own_sem.at[0])
    put.start()

    def first_q(mask, rel):
        return pl.multiple_of(((aa ^ mask) * n_col + ((col // plan.near) ^ rel) * plan.near) * q_local, depth)

    def bd_piece(rel, part, mask):
        return bd_all.at[pl.ds(first_q(mask, rel), depth), pl.ds(part * half, half)]

    def t_piece(part, mask):
        return t_all.at[part, pl.ds((aa ^ mask) * d_local, d_local)]

    def t_source(part, mask):
        return amplitudes.at[part] if mask == 0 else t_piece(part, mask)

    place = (aa, col)
    exchanges = []
    for rel in range(plan.halves):
        piece = functools.partial(bd_piece, rel)
        exchanges.append(Exchange(plan, piece, piece, x_send.at[rel], x_recv.at[rel], place))
    exchange_t = Exchange(plan, t_source, t_piece, x_send.at[plan.halves], x_recv.at[plan.halves], place)

    def begin_half(rel):
        for step in range(max(1, rel * plan.near), (rel + 1) * plan.near):
            along[step - 1].wait_recv()
        if rel == 0:
            put.wait()
        exchanges[rel].own()

    last = len(plan.phases) - 1
    events = [(0, 2, lambda: exchanges[0].wave(0))]
    if plan.halves > 1:
        for rel in range(1, plan.halves):
            events.append((0, 6, functools.partial(begin_half, rel)))
    events.append((1, -1, lambda: exchanges[0].wave(1)))
    events.append((1, 0, lambda: exchanges[0].wave(2)))
    for rel in range(1, plan.halves):
        events.append((1, 2, functools.partial(exchanges[rel].wave, 0)))
        events.append((1, 4, functools.partial(exchanges[rel].wave, 1)))
    events.append((1, 4, exchange_t.own))
    for rel in range(1, plan.halves):
        events.append((1, 7, functools.partial(exchanges[rel].wave, 2)))
    events.append((2, 3, lambda: exchange_t.wave(0)))
    events.append((2, 6, lambda: exchange_t.wave(1)))

    def run_events(phase, at):
        for when, step, act in events:
            if when == phase and step == at:
                act()

    def loads(phase, index, slot):
        rows = plan.rows[phase]
        found = []
        for at, (mask, rel) in enumerate(plan.phases[phase]):
            found.append(
                pltpu.make_async_copy(
                    fit_ac.at[pl.ds(index * rows, rows), :, pl.ds(first_q(mask, rel), depth)],
                    blocks_a.at[slot, at % 4, pl.ds(at // 4 * rows, rows)],
                    a_sem.at[slot, at],
                )
            )
        return found

    def fetch(phase, index, slot):
        for one in loads(phase, index, slot):
            one.start()

    def prepare(phase, base):
        pieces = plan.phases[phase]
        for mask, rel in pieces:
            if mask & 1:
                exchanges[rel].core(mask)
        starts = [first_q(mask, rel) for mask, rel in pieces]

        def source(at):
            row = starts[0]
            for one in range(1, len(starts)):
                row = jnp.where(at == one, starts[one], row)
            slot = lax.rem(at, 2)
            row = pl.multiple_of(row, depth)
            return pltpu.make_async_copy(bd_all.at[pl.ds(row, depth)], stage.at[slot], stage_sem.at[slot])

        source(jnp.int32(0)).start()

        @pl.loop(0, len(pieces))
        def _(at):
            @pl.when(at + 1 < len(pieces))
            def _():
                source(at + 1).start()

            source(at).wait()
            turned[...] = stage[lax.rem(at, 2)].T
            lanes = pl.ds(pl.multiple_of(base + at * depth, depth), depth)
            for k in range(plan.blocks):
                for d in range(0, plan.d_size, 2):
                    first = k * plan.b_size * plan.d_size + d
                    value = jnp.concatenate(
                        [turned[pl.ds(first + one, plan.b_size, stride=plan.d_size), :] for one in range(2)], axis=0
                    )
                    top, rest = split(value)
                    to = (pl.ds((k * plan.d_size + d) * plan.b_size, 2 * plan.b_size), lanes)
                    high[to] = (top.astype(F32) * SCALE).astype(BF16)
                    low8[to] = (rest * B_LO).astype(F8)
                    high8[to] = (value * B_HI).astype(F8)

    dot = functools.partial(lax.dot_general, dimension_numbers=NT, preferred_element_type=F32)

    def multiply(phase, base, index):
        pieces, rows = plan.phases[phase], plan.rows[phase]
        slot = lax.rem(index, 2)
        for one in loads(phase, index, slot):
            one.wait()
        parts = [
            blocks_a[slot, at % 4, at // 4 * rows : at // 4 * rows + rows].reshape(rows * plan.c_local, depth)
            for at in range(len(pieces))
        ]
        value = jnp.concatenate(parts, axis=1)
        top, rest = split(value)
        lanes = slice(base, base + depth * len(pieces))
        made_here = dot(high[:, lanes], top)
        made_here += dot(low8[:, lanes], (value * A_HI).astype(F8))
        made_here += dot(high8[:, lanes], (rest * A_LO).astype(F8))
        count = plan.blocks * plan.d_size
        for row in range(rows):
            one = made_here[:, row * plan.c_local : (row + 1) * plan.c_local]
            one = one.reshape(count, plan.b_size, plan.c_local)
            at = index * rows + row
            if phase == 0:
                acc[:, at] = one
            else:
                acc[:, at] += one

    begin_half(0)
    fetch(0, 0, 0)
    base = 0
    for phase in range(last):
        run_events(phase, -1)
        prepare(phase, base)
        steps = plan.a_local // plan.rows[phase]

        @pl.loop(0, steps)
        def _(index, phase=phase, base=base, steps=steps):
            @pl.when(index + 1 < steps)
            def _():
                fetch(phase, index + 1, lax.rem(index + 1, 2))

            @pl.when(index + 1 == steps)
            def _():
                fetch(phase + 1, 0, steps % 2)

            for at in range(steps):
                if any(when == phase and step == at for when, step, _ in events):
                    pl.when(index == at)(functools.partial(run_events, phase, at))
            multiply(phase, base, index)

        for at in range(steps, 8):
            run_events(phase, at)
        base += depth * len(plan.phases[phase])

    for at in range(-1, 8):
        run_events(last, at)
    prepare(last, base)
    span = d_local * plan.c_local

    def prepare_t():
        if last < 2:
            exchange_t.wave(0)
            exchange_t.wave(1)
        exchange_t.wave(2)
        keep.wait()
        for mask in range(1, n_aa, 2):
            exchange_t.core(mask)
        count = plan.blocks * n_aa

        def source(at):
            slot = lax.rem(at, 2)
            src = t_all.at[at // n_aa, pl.ds(lax.rem(at, n_aa) * d_local, d_local)]
            return pltpu.make_async_copy(src, t_stage.at[slot], t_sem.at[slot])

        source(jnp.int32(0)).start()

        @pl.loop(0, count)
        def _(at):
            @pl.when(at + 1 < count)
            def _():
                source(at + 1).start()

            source(at).wait()
            value = t_stage[lax.rem(at, 2)].reshape(span, plan.pairs) * UNDO
            top, rest = split(value)
            to = (at // n_aa, pl.ds(pl.multiple_of(lax.rem(at, n_aa) * span, span), span))
            t_high[to] = top
            t_low[to] = rest.astype(BF16)

    group, rows = plan.group, plan.rows[last]
    groups, inner = plan.a_local // group, plan.group // rows
    plain = functools.partial(jnp.dot, preferred_element_type=F32)
    wide = 8 if plan.c_local % LANES == 0 else 1

    def ladder(k, which):
        total = None
        for d in range(0, plan.d_size, wide):
            parts = []
            for one in range(d, d + wide):
                part = acc[k * plan.d_size + one, pl.ds(which * group, group)]
                parts.append(part.reshape(group * plan.b_size, plan.c_local))
            x_high, x_low = split(jnp.concatenate(parts, axis=1) if wide > 1 else parts[0])
            at = slice(d * plan.c_local, (d + wide) * plan.c_local)
            t_top, t_rest = t_high[k, at], t_low[k, at]
            term = plain(x_high, t_top) + plain(x_low.astype(BF16), t_top) + plain(x_high, t_rest)
            total = term if total is None else total + term
        return total

    def away(which, step):
        slot = lax.rem(which, 2)
        to = col ^ step
        src = ready.at[slot, :, pl.ds(to * plan.b_out, plan.b_out)]
        dst = sums.at[step, :, :, pl.ds(which * group, group)]
        if step == 0:
            return pltpu.make_async_copy(src, dst, r_own.at[slot])
        return pltpu.make_async_remote_copy(
            src_ref=src,
            dst_ref=dst,
            send_sem=r_send.at[slot, step - 1],
            recv_sem=r_recv.at[which, step - 1],
            device_id=(aa, to),
            device_id_type=MESH,
        )

    def left(which):
        away(which, 0).wait()
        for step in range(1, n_col):
            away(which, step).wait_send()

    steps = groups * inner

    @pl.loop(0, groups)
    def _(which):
        @pl.loop(0, inner)
        def _(sub):
            index = which * inner + sub

            @pl.when(index + 1 < steps)
            def _():
                fetch(last, index + 1, lax.rem(index + 1, 2))

            multiply(last, base, index)

        pl.when(which == 0)(prepare_t)

        @pl.when(which >= 2)
        def _():
            left(which - 2)

        slot = lax.rem(which, 2)

        @pl.loop(0, plan.blocks)
        def _(k):
            total = ladder(k, which)
            for at in range(0, plan.pairs, LANES):
                made[...] = total[:, at : at + LANES]
                for b in range(plan.b_size):
                    ready[slot, k, b, :, at : at + LANES] = made[pl.ds(b, group, stride=plan.b_size), :]

        for step in range(1, n_col):
            away(which, step).start()
        away(which, 0).start()

    for which in range(max(0, groups - 2), groups):
        left(jnp.int32(which))
    for one in along:
        one.wait_send()
    for one in exchanges + [exchange_t]:
        one.finish()
    for which in range(groups):
        for step in range(1, n_col):
            away(jnp.int32(which), step).wait_recv()


def shards(n_aa, n_col, fit_ac, fit_bd, amplitudes):
    plan = Plan(n_aa, n_col, fit_ac, fit_bd, amplitudes)
    columns, count_q, c_local, pairs = plan.columns, plan.count_q, plan.c_local, plan.pairs
    dma, any_ = pltpu.SemaphoreType.DMA, pl.BlockSpec(memory_space=pl.ANY)
    groups = plan.a_local // plan.group
    most = max(len(phase) for phase in plan.phases)
    sums, _, _ = pl.pallas_call(
        functools.partial(kernel, plan),
        in_specs=[any_] * 3,
        out_specs=[any_] * 3,
        out_shape=[
            jax.ShapeDtypeStruct((n_col, plan.blocks, plan.b_out, plan.a_local, pairs), F32),
            jax.ShapeDtypeStruct((count_q, columns), F32),
            jax.ShapeDtypeStruct((plan.blocks, plan.d_size, c_local, pairs), F32),
        ],
        scratch_shapes=[
            pltpu.VMEM((plan.blocks * plan.d_size, plan.a_local, plan.b_size, c_local), F32),
            pltpu.VMEM((columns, count_q), BF16),
            pltpu.VMEM((columns, count_q), F8),
            pltpu.VMEM((columns, count_q), F8),
            pltpu.VMEM((plan.blocks, plan.d_size * c_local, pairs), BF16),
            pltpu.VMEM((plan.blocks, plan.d_size * c_local, pairs), BF16),
            pltpu.VMEM((2, 4, 8, c_local, plan.depth), F32),
            pltpu.VMEM((2, plan.depth, columns), F32),
            pltpu.VMEM((columns, plan.depth), F32),
            pltpu.VMEM((2, plan.d_local, c_local, pairs), F32),
            pltpu.VMEM((plan.group * plan.b_size, LANES), F32),
            pltpu.VMEM((2, plan.blocks, plan.b_size, plan.group, pairs), F32),
            dma((2, most)),
            dma((2,)),
            dma((2,)),
            dma((2,)),
            dma((n_col - 1,)),
            dma((n_col - 1,)),
            dma((plan.halves + 1, plan.moves)),
            dma((plan.halves + 1, plan.moves)),
            dma((2, n_col - 1)),
            dma((groups, n_col - 1)),
            dma((2,)),
        ],
        compiler_params=pltpu.CompilerParams(vmem_limit_bytes=VMEM_LIMIT, collective_id=0, has_side_effects=True),
    )(fit_ac, fit_bd, amplitudes)
    return sums.sum(axis=0)


def solution(mesh):
    placed = (P("aa", "col", None), P(("aa", "col"), None), P(None, "aa", "col", None))
    body = functools.partial(shards, mesh.shape["aa"], mesh.shape["col"])
    return jax.shard_map(
        body, mesh=mesh, in_specs=placed, out_specs=P(None, "col", "aa", None), check_vma=False
    )
```

profile of v0, /device:TPU:0, one launch (start us, length us, event | category | flops | bytes accessed | tf_op | source)
XLA Modules:
  0.0 162.0 jit_solution(733527301740262309)
XLA Ops:
  0.0 159.4 %shard_map.37 = (f32[4,2,4,64,256]{4,3,2,1,0:T(8,128)}, f32[2048,1024]{1,0:T(8,128)}, f32[2,32,128,256]{3,2,1,0:T(8,128)}) custom-call(f32[64,128,2048]{2,1,0:T(8,128)} %fit_ac.1, f32[64,1024]{1,0:T(8,128)} %fit_bd.1, f32[2,4,128,256]{3,2,1,0:T(8,128)} %amplitudes.1), custom_call_target="tpu_custom_call" | custom-call | tf_op jit(solution)/shard_map/pallas_call | solution.py:423
  159.4 2.6 %reduce_sum.9 = f32[2,4,64,256]{3,2,1,0:T(8,128)} reduce(f32[4,2,4,64,256]{4,3,2,1,0:T(8,128)} %get-tuple-element.6, f32[]{:T(128)} %constant.0.clone.1), dimensions={0}, to_apply=%region_0.0 | reduce | flops 393216 | bytes 2621444 | tf_op jit(solution)/shard_map/reduce_sum | solution.py:459
where the time goes:
time: 163 us; the launch traced here: 162 us
  Pallas kernels  159 us (98%)
  other arithmetic  2.59 us (2%)
    pallas_call x1, Pallas kernels, shards(): pl.pallas_call(functools.partial(kernel, plan), in_specs=[any_] * 3, out_...  159 us

commit v1 on v0

v1 whole, which is shorter than its diff:
```python
import functools

import jax
import jax.numpy as jnp
from jax import lax
from jax.experimental import pallas as pl
from jax.experimental.pallas import tpu as pltpu
from jax.sharding import PartitionSpec as P

F32 = jnp.float32
BF16 = jnp.bfloat16
F8 = jnp.float8_e4m3fn
NT = (((1,), (1,)), ((), ()))
MESH = pl.DeviceIdType.MESH
VMEM_LIMIT = 67_000_000

A_HI, A_LO, B_HI, B_LO = 2.0**11, 2.0**20, 2.0**5, 2.0**14
SCALE, UNDO = 2.0**25, 2.0**-25
LANES = 128
PARTS = 2


def split(value):
    high = value.astype(BF16)
    return high, value - high.astype(F32)


class Plan:
    def __init__(self, n_aa, n_col, fit_ac, fit_bd, amplitudes):
        self.n_aa, self.n_col = n_aa, n_col
        self.a_local, self.c_local, self.count_q = fit_ac.shape
        self.blocks, self.d_local, _, self.pairs = amplitudes.shape
        self.q_local, self.columns = fit_bd.shape
        self.d_size = self.d_local * n_aa
        self.b_size = self.columns // (self.blocks * self.d_size)
        self.b_out = self.b_size // n_col
        self.near = min(n_col, max(1, LANES // self.q_local))
        self.halves = n_col // self.near
        self.depth = self.near * self.q_local
        self.far = [1 << bit for bit in range(1, n_aa.bit_length() - 1)]
        self.orders = [self.far, self.far[::-1]]
        masks = [mask for mask in range(0, n_aa, 2)]
        ones = [m for m in masks if m.bit_count() == 1]
        more = [m for m in masks if m.bit_count() > 1]
        rest = range(1, self.halves)
        own = [(m, 0) for m in (0,)]
        self.phases = [own, [(m, 0) for m in ones], [(m, 0) for m in more] + [(0, r) for r in rest]]
        self.phases.append([(m, r) for r in rest for m in ones + more])
        self.phases = [[(m ^ core, r) for core in (0, 1) for m, r in phase] for phase in self.phases if phase]
        self.group = min(self.a_local, 16)
        self.tail = self.group // 2
        self.rows = [8 if len(phase) <= 4 else 4 for phase in self.phases]
        self.waves = [[], [], []]
        for part, order in enumerate(self.orders):
            for mask in sorted(masks[1:], key=lambda m: m.bit_count()):
                stage = max(order.index(bit) for bit in self.far if bit & mask)
                wave = 2 if mask.bit_count() > 1 else (0 if stage == 0 else 1)
                self.waves[wave].append((part, mask, order[stage], order[stage + 1 :]))
        self.waves[2].sort(key=lambda one: one[1].bit_count())
        self.t_each = -(-n_aa * self.rows[-1] // self.group)
        self.moves = PARTS * (n_aa // 2 - 1 + n_aa // 2)


class Exchange:
    def __init__(self, plan, source, target, send, recv, place):
        self.plan, self.source, self.target = plan, source, target
        self.send, self.recv, self.place, self.keys = send, recv, place, {}

    def copy(self, part, mask, bit):
        index = self.keys.setdefault((part, mask, bit), len(self.keys))
        aa, col = self.place
        return pltpu.make_async_remote_copy(
            src_ref=self.source(part, mask),
            dst_ref=self.target(part, mask),
            send_sem=self.send.at[index],
            recv_sem=self.recv.at[index],
            device_id=(aa ^ bit, col),
            device_id_type=MESH,
        )

    def own(self):
        for stage in range(len(self.plan.far)):
            for part, order in enumerate(self.plan.orders):
                self.copy(part, 0, order[stage]).start()
        for part in range(PARTS):
            self.copy(part, 0, 1).start()

    def wave(self, which):
        for part, mask, bit, later in self.plan.waves[which]:
            self.copy(part, mask ^ bit, bit).wait_recv()
            for further in later:
                self.copy(part, mask, further).start()
            self.copy(part, mask, 1).start()

    def core(self, mask):
        for part in range(PARTS):
            self.copy(part, mask ^ 1, 1).wait_recv()

    def finish(self):
        for key in list(self.keys):
            self.copy(*key).wait_send()


def kernel(plan, fit_ac, fit_bd, amplitudes, sums, bd_all, t_all, *refs):
    count = len(plan.phases)
    highs, lows8, highs8 = refs[:count], refs[count : 2 * count], refs[2 * count : 3 * count]
    acc, t_high, t_low, blocks_a, stage, turned, t_stage, made, ready = refs[3 * count : 3 * count + 9]
    a_sem, own_sem, stage_sem, t_sem, z_send, z_recv, x_send, x_recv, r_send, r_recv, r_own = refs[3 * count + 9 :]
    aa, col = lax.axis_index("aa").astype(jnp.int32), lax.axis_index("col").astype(jnp.int32)
    n_col, n_aa = plan.n_col, plan.n_aa
    q_local, depth, d_local = plan.q_local, plan.depth, plan.d_local
    half = plan.columns // PARTS

    barrier = pltpu.get_barrier_semaphore()
    peers = [(aa, col ^ step) for step in range(1, n_col)] + [(aa ^ bit, col) for bit in [1] + plan.far]
    for peer in peers:
        pl.semaphore_signal(barrier, inc=1, device_id=peer, device_id_type=MESH)

    mine = pl.ds(pl.multiple_of((aa * n_col + col) * q_local, q_local), q_local)
    take = pltpu.make_async_copy(fit_bd, stage.at[0, pl.ds(0, q_local)], own_sem.at[0])
    take.start()
    keep = pltpu.make_async_copy(amplitudes, t_all.at[:, pl.ds(aa * d_local, d_local)], own_sem.at[1])
    keep.start()
    pl.semaphore_wait(barrier, len(peers))

    along = []
    for step in range(1, n_col):
        along.append(
            pltpu.make_async_remote_copy(
                src_ref=fit_bd,
                dst_ref=bd_all.at[mine],
                send_sem=z_send.at[step - 1],
                recv_sem=z_recv.at[step - 1],
                device_id=(aa, col ^ step),
                device_id_type=MESH,
            )
        )
        if step < plan.near:
            along[-1].start()
    take.wait()
    put = pltpu.make_async_copy(stage.at[0, pl.ds(0, q_local)], bd_all.at[mine], own_sem.at[0])
    put.start()

    def first_q(mask, rel):
        return pl.multiple_of(((aa ^ mask) * n_col + ((col // plan.near) ^ rel) * plan.near) * q_local, depth)

    def bd_piece(rel, part, mask):
        return bd_all.at[pl.ds(first_q(mask, rel), depth), pl.ds(part * half, half)]

    def t_piece(part, mask):
        return t_all.at[part, pl.ds((aa ^ mask) * d_local, d_local)]

    def t_source(part, mask):
        return amplitudes.at[part] if mask == 0 else t_piece(part, mask)

    place = (aa, col)
    exchanges = []
    for rel in range(plan.halves):
        piece = functools.partial(bd_piece, rel)
        exchanges.append(Exchange(plan, piece, piece, x_send.at[rel], x_recv.at[rel], place))
    exchange_t = Exchange(plan, t_source, t_piece, x_send.at[plan.halves], x_recv.at[plan.halves], place)

    def begin_half(rel):
        for step in range(max(1, rel * plan.near), (rel + 1) * plan.near):
            along[step - 1].wait_recv()
        if rel == 0:
            for step in range(plan.near, n_col):
                along[step - 1].start()
            put.wait()
        exchanges[rel].own()

    last = len(plan.phases) - 1
    events = [(0, 4, lambda: exchanges[0].wave(0)), (0, 7, exchange_t.own)]
    events.append((1, -1, lambda: exchanges[0].wave(1)))
    events.append((1, 0, lambda: exchanges[0].wave(2)))
    for rel in range(1, plan.halves):
        events.append((1, 2, functools.partial(begin_half, rel)))
        events.append((1, 5, functools.partial(exchanges[rel].wave, 0)))
    events.append((1, 7, lambda: exchange_t.wave(0)))
    for rel in range(1, plan.halves):
        events.append((2, 0, functools.partial(exchanges[rel].wave, 1)))
        events.append((2, 2, functools.partial(exchanges[rel].wave, 2)))
    events.append((2, 4, lambda: exchange_t.wave(1)))

    def run_events(phase, at):
        for when, step, act in events:
            if when == phase and step == at:
                act()

    def loads(phase, index, slot):
        rows = plan.rows[phase]
        found = []
        for at, (mask, rel) in enumerate(plan.phases[phase]):
            found.append(
                pltpu.make_async_copy(
                    fit_ac.at[pl.ds(index * rows, rows), :, pl.ds(first_q(mask, rel), depth)],
                    blocks_a.at[slot, at % 4, pl.ds(at // 4 * rows, rows)],
                    a_sem.at[slot, at],
                )
            )
        return found

    def fetch(phase, index, slot):
        for one in loads(phase, index, slot):
            one.start()

    def bring(phase, at):
        pieces = plan.phases[phase]
        row = jnp.int32(0)
        for one, (mask, rel) in enumerate(pieces):
            row = jnp.where(at == one, first_q(mask, rel), row)
        slot = lax.rem(at, 2)
        return pltpu.make_async_copy(
            bd_all.at[pl.ds(pl.multiple_of(row, depth), depth)], stage.at[slot], stage_sem.at[slot]
        )

    def start_bring(phase, at):
        pieces = plan.phases[phase]
        for one, (mask, rel) in enumerate(pieces):
            if mask & 1:
                pl.when(at == one)(functools.partial(exchanges[rel].core, mask))

        @pl.when(at < len(pieces))
        def _():
            bring(phase, at).start()

    def arrange(phase, at):
        turned[...] = stage[lax.rem(at, 2)].T
        lanes = pl.ds(pl.multiple_of(at * depth, depth), depth)
        for k in range(plan.blocks):
            for d in range(0, plan.d_size, 2):
                first = k * plan.b_size * plan.d_size + d
                value = jnp.concatenate(
                    [turned[pl.ds(first + one, plan.b_size, stride=plan.d_size), :] for one in range(2)], axis=0
                )
                top, rest = split(value)
                to = (pl.ds((k * plan.d_size + d) * plan.b_size, 2 * plan.b_size), lanes)
                highs[phase][to] = (top.astype(F32) * SCALE).astype(BF16)
                lows8[phase][to] = (rest * B_LO).astype(F8)
                highs8[phase][to] = (value * B_HI).astype(F8)

    def prepare(phase):
        start_bring(phase, jnp.int32(0))
        start_bring(phase, jnp.int32(1))

        @pl.loop(0, len(plan.phases[phase]))
        def _(at):
            bring(phase, at).wait()
            arrange(phase, at)
            start_bring(phase, at + 2)

    dot = functools.partial(lax.dot_general, dimension_numbers=NT, preferred_element_type=F32)

    def multiply(phase, index):
        pieces, rows = plan.phases[phase], plan.rows[phase]
        slot = lax.rem(index, 2)
        for one in loads(phase, index, slot):
            one.wait()
        parts = [
            blocks_a[slot, at % 4, at // 4 * rows : at // 4 * rows + rows].reshape(rows * plan.c_local, depth)
            for at in range(len(pieces))
        ]
        value = jnp.concatenate(parts, axis=1)
        top, rest = split(value)
        made_here = dot(highs[phase][...], top)
        made_here += dot(lows8[phase][...], (value * A_HI).astype(F8))
        made_here += dot(highs8[phase][...], (rest * A_LO).astype(F8))
        count = plan.blocks * plan.d_size
        for row in range(rows):
            one = made_here[:, row * plan.c_local : (row + 1) * plan.c_local]
            one = one.reshape(count, plan.b_size, plan.c_local)
            at = index * rows + row
            if phase == 0:
                acc[:, at] = one
            else:
                acc[:, at] += one

    begin_half(0)
    fetch(0, 0, 0)
    prepared = False
    for phase in range(last):
        run_events(phase, -1)
        if not prepared:
            prepare(phase)
        steps, ahead = plan.a_local // plan.rows[phase], len(plan.phases[phase + 1])
        prepared = phase > 0 and ahead < steps
        plain_steps = steps - ahead if prepared else steps

        def before(index, low, high, phase=phase, steps=steps):
            @pl.when(index + 1 < steps)
            def _():
                fetch(phase, index + 1, lax.rem(index + 1, 2))

            @pl.when(index + 1 == steps)
            def _():
                fetch(phase + 1, 0, steps % 2)

            for at in range(low, high):
                if any(when == phase and step == at for when, step, _ in events):
                    pl.when(index == at)(functools.partial(run_events, phase, at))

        @pl.loop(0, plain_steps)
        def _(index, phase=phase, before=before, plain_steps=plain_steps):
            before(index, 0, plain_steps)
            multiply(phase, index)

        if prepared:
            start_bring(phase + 1, jnp.int32(0))

            @pl.loop(plain_steps, steps)
            def _(index, phase=phase, before=before, plain_steps=plain_steps, steps=steps):
                before(index, plain_steps, steps)
                at = index - plain_steps
                bring(phase + 1, at).wait()
                start_bring(phase + 1, at + 1)
                multiply(phase, index)
                arrange(phase + 1, at)

        for at in range(steps, 8):
            run_events(phase, at)

    for at in range(-1, 8):
        run_events(last, at)
    if not prepared:
        prepare(last)
    span = d_local * plan.c_local

    each = plan.t_each

    def t_copy(k, mask):
        slot = lax.rem(mask, 2 * each)
        src = t_all.at[k, pl.ds((aa ^ mask) * d_local, d_local)]
        return pltpu.make_async_copy(src, t_stage.at[slot], t_sem.at[slot])

    def t_arrange(k, mask):
        value = t_stage[lax.rem(mask, 2 * each)].reshape(span, plan.pairs) * UNDO
        top, rest = split(value)
        to = (k, pl.ds(pl.multiple_of((aa ^ mask) * span, span), span))
        t_high[to] = top
        t_low[to] = rest.astype(BF16)

    def t_begin(k, at):
        for one in range(each):
            t_copy(k, at * each + one).start()

    def t_end(k, at):
        for one in range(each):
            t_copy(k, at * each + one).wait()

    def t_work(k, at):
        for one in range(each):
            t_arrange(k, at * each + one)

    def t_gather(masks):
        for mask in masks:
            if mask & 1:
                exchange_t.core(mask)

    group, rows = plan.group, plan.rows[last]
    inner = group // rows
    plain = functools.partial(jnp.dot, preferred_element_type=F32)
    wide = 8 if plan.c_local % LANES == 0 else 1

    def ladder(k, start, size):
        total = None
        for d in range(0, plan.d_size, wide):
            parts = []
            for one in range(d, d + wide):
                part = acc[k * plan.d_size + one, pl.ds(start, size)]
                parts.append(part.reshape(size * plan.b_size, plan.c_local))
            x_high, x_low = split(jnp.concatenate(parts, axis=1) if wide > 1 else parts[0])
            at = slice(d * plan.c_local, (d + wide) * plan.c_local)
            t_top, t_rest = t_high[k, at], t_low[k, at]
            term = plain(x_high, t_top) + plain(x_low.astype(BF16), t_top) + plain(x_high, t_rest)
            total = term if total is None else total + term
        return total

    def away(start, size, number, step):
        to = col ^ step
        slot = lax.rem(number, 2)
        src = ready.at[slot, :, pl.ds(to * plan.b_out, plan.b_out), pl.ds(0, size)]
        dst = sums.at[step, :, :, pl.ds(start, size)]
        if step == 0:
            return pltpu.make_async_copy(src, dst, r_own.at[number])
        return pltpu.make_async_remote_copy(
            src_ref=src,
            dst_ref=dst,
            send_sem=r_send.at[number, step - 1],
            recv_sem=r_recv.at[number, step - 1],
            device_id=(aa, to),
            device_id_type=MESH,
        )

    total_steps = plan.a_local // rows

    def contract(index):
        @pl.when(index + 1 < total_steps)
        def _():
            fetch(last, index + 1, lax.rem(index + 1, 2))

        multiply(last, index)

    def left(start, size, number):
        away(start, size, number, 0).wait()
        for step in range(1, n_col):
            away(start, size, number, step).wait_send()

    def finish(start, size, number):
        slot = lax.rem(number, 2)

        @pl.loop(0, plan.blocks)
        def _(k):
            total = ladder(k, start, size)
            for at in range(0, plan.pairs, LANES):
                made[0 : size * plan.b_size] = total[:, at : at + LANES]
                for b in range(plan.b_size):
                    ready[slot, k, b, 0:size, at : at + LANES] = made[pl.ds(b, size, stride=plan.b_size), :]

        for step in range(1, n_col):
            away(start, size, number, step).start()
        away(start, size, number, 0).start()

    if last < 2:
        exchange_t.wave(0)
        exchange_t.wave(1)
    keep.wait()
    early = each * (inner - 1)
    late = not any((mask & ~1).bit_count() > 1 for mask in range(early))
    if not late:
        exchange_t.wave(2)
        early = n_aa
    t_gather(range(early))
    t_begin(0, 0)

    @pl.loop(0, inner)
    def _(index):
        if late:

            @pl.when(index == inner - 2)
            def _():
                exchange_t.wave(2)
                t_gather(range(early, n_aa))

        @pl.when(index + 1 < inner)
        def _():
            t_begin(0, index + 1)

        t_end(0, index)

        @pl.when(index + 1 < total_steps)
        def _():
            fetch(last, index + 1, lax.rem(index + 1, 2))

        multiply(last, index)
        t_work(0, index)

    t_begin(1, 0)

    @pl.loop(0, inner)
    def _(index):
        @pl.when(index + 1 < inner)
        def _():
            t_begin(1, index + 1)

        t_end(1, index)
        t_work(1, index)

    bulk = plan.a_local // group - 1

    @pl.loop(0, bulk)
    def _(which):
        @pl.when(which > 0)
        def _():
            @pl.loop(0, inner)
            def _(sub):
                contract(which * inner + sub)

        @pl.when(which >= 2)
        def _():
            left(pl.multiple_of((which - 2) * group, group), group, which - 2)

        finish(pl.multiple_of(which * group, group), group, which)

    tail, tail_inner = plan.tail, plan.tail // rows
    sent = [(which * group, group, jnp.int32(which)) for which in range(bulk)]
    sent += [(bulk * group + at * tail, tail, jnp.int32(bulk + at)) for at in range(2)]
    for at in range(2):

        @pl.loop(0, tail_inner)
        def _(sub, at=at):
            contract(bulk * inner + at * tail_inner + sub)

        if bulk + at >= 2:
            left(*sent[bulk + at - 2])
        finish(*sent[bulk + at])

    for one in sent[-2:]:
        left(*one)
    for one in along:
        one.wait_send()
    for one in exchanges + [exchange_t]:
        one.finish()
    for start, size, number in sent:
        for step in range(1, n_col):
            away(start, size, number, step).wait_recv()


def shards(n_aa, n_col, fit_ac, fit_bd, amplitudes):
    plan = Plan(n_aa, n_col, fit_ac, fit_bd, amplitudes)
    columns, count_q, c_local, pairs = plan.columns, plan.count_q, plan.c_local, plan.pairs
    dma, any_ = pltpu.SemaphoreType.DMA, pl.BlockSpec(memory_space=pl.ANY)
    sends = plan.a_local // plan.group + 1
    widths = [plan.depth * len(phase) for phase in plan.phases]
    most = max(len(phase) for phase in plan.phases)
    sums, _, _ = pl.pallas_call(
        functools.partial(kernel, plan),
        in_specs=[any_] * 3,
        out_specs=[any_] * 3,
        out_shape=[
            jax.ShapeDtypeStruct((n_col, plan.blocks, plan.b_out, plan.a_local, pairs), F32),
            jax.ShapeDtypeStruct((count_q, columns), F32),
            jax.ShapeDtypeStruct((plan.blocks, plan.d_size, c_local, pairs), F32),
        ],
        scratch_shapes=[pltpu.VMEM((columns, width), BF16) for width in widths]
        + [pltpu.VMEM((columns, width), F8) for width in widths * 2]
        + [
            pltpu.VMEM((plan.blocks * plan.d_size, plan.a_local, plan.b_size, c_local), F32),
            pltpu.VMEM((plan.blocks, plan.d_size * c_local, pairs), BF16),
            pltpu.VMEM((plan.blocks, plan.d_size * c_local, pairs), BF16),
            pltpu.VMEM((2, 4, 8, c_local, plan.depth), F32),
            pltpu.VMEM((2, plan.depth, columns), F32),
            pltpu.VMEM((columns, plan.depth), F32),
            pltpu.VMEM((2 * plan.t_each, plan.d_local, c_local, pairs), F32),
            pltpu.VMEM((plan.group * plan.b_size, LANES), F32),
            pltpu.VMEM((2, plan.blocks, plan.b_size, plan.group, pairs), F32),
            dma((2, most)),
            dma((2,)),
            dma((2,)),
            dma((2 * plan.t_each,)),
            dma((n_col - 1,)),
            dma((n_col - 1,)),
            dma((plan.halves + 1, plan.moves)),
            dma((plan.halves + 1, plan.moves)),
            dma((sends, n_col - 1)),
            dma((sends, n_col - 1)),
            dma((sends,)),
        ],
        compiler_params=pltpu.CompilerParams(vmem_limit_bytes=VMEM_LIMIT, collective_id=0, has_side_effects=True),
    )(fit_ac, fit_bd, amplitudes)
    return sums.sum(axis=0)


def solution(mesh):
    placed = (P("aa", "col", None), P(("aa", "col"), None), P(None, "aa", "col", None))
    body = functools.partial(shards, mesh.shape["aa"], mesh.shape["col"])
    return jax.shard_map(
        body, mesh=mesh, in_specs=placed, out_specs=P(None, "col", "aa", None), check_vma=False
    )
```

time: 163 us -> 161 us (0.988)
  no operation moved by 1% of the time
where the time goes in v1:
time: 161 us
  Pallas kernels  158 us (98%)
  other arithmetic  2.59 us (2%)
    pallas_call x1, Pallas kernels, shards(): pl.pallas_call(functools.partial(kernel, plan), in_specs=[any_] * 3, out_...  158 us

profile of v1, /device:TPU:0, one launch (start us, length us, event | category | flops | bytes accessed | tf_op | source)
XLA Modules:
  0.0 160.7 jit_solution(3479764807918458419)
XLA Ops:
  0.0 158.1 %shard_map.37 = (f32[4,2,4,64,256]{4,3,2,1,0:T(8,128)}, f32[2048,1024]{1,0:T(8,128)}, f32[2,32,128,256]{3,2,1,0:T(8,128)}) custom-call(f32[64,128,2048]{2,1,0:T(8,128)} %fit_ac.1, f32[64,1024]{1,0:T(8,128)} %fit_bd.1, f32[2,4,128,256]{3,2,1,0:T(8,128)} %amplitudes.1), custom_call_target="tpu_custom_call" | custom-call | tf_op jit(solution)/shard_map/pallas_call | solution.py:515
  158.1 2.6 %reduce_sum.9 = f32[2,4,64,256]{3,2,1,0:T(8,128)} reduce(f32[4,2,4,64,256]{4,3,2,1,0:T(8,128)} %get-tuple-element.6, f32[]{:T(128)} %constant.0.clone.1), dimensions={0}, to_apply=%region_0.0 | reduce | flops 393216 | bytes 2621444 | tf_op jit(solution)/shard_map/reduce_sum | solution.py:550

commit v2 on v1

--- a/solution.py
+++ b/solution.py
@@ -78,12 +78,13 @@
             device_id_type=MESH,
         )
 
-    def own(self):
-        for stage in range(len(self.plan.far)):
+    def own(self, first=0, last=None):
+        for stage in range(len(self.plan.far))[first:last]:
             for part, order in enumerate(self.plan.orders):
                 self.copy(part, 0, order[stage]).start()
-        for part in range(PARTS):
-            self.copy(part, 0, 1).start()
+        if first == 0:
+            for part in range(PARTS):
+                self.copy(part, 0, 1).start()
 
     def wave(self, which):
         for part, mask, bit, later in self.plan.waves[which]:
@@ -170,17 +171,18 @@
         exchanges[rel].own()
 
     last = len(plan.phases) - 1
-    events = [(0, 4, lambda: exchanges[0].wave(0)), (0, 7, exchange_t.own)]
+    events = [(0, 4, lambda: exchanges[0].wave(0)), (0, 7, lambda: exchange_t.own(0, 1))]
     events.append((1, -1, lambda: exchanges[0].wave(1)))
     events.append((1, 0, lambda: exchanges[0].wave(2)))
     for rel in range(1, plan.halves):
         events.append((1, 2, functools.partial(begin_half, rel)))
-        events.append((1, 5, functools.partial(exchanges[rel].wave, 0)))
-    events.append((1, 7, lambda: exchange_t.wave(0)))
+        events.append((1, 6, functools.partial(exchanges[rel].wave, 0)))
+    events.append((1, 6, lambda: exchange_t.own(1)))
+    events.append((1, 6, lambda: exchange_t.wave(0)))
     for rel in range(1, plan.halves):
         events.append((2, 0, functools.partial(exchanges[rel].wave, 1)))
         events.append((2, 2, functools.partial(exchanges[rel].wave, 2)))
-    events.append((2, 4, lambda: exchange_t.wave(1)))
+    events.append((2, 5, lambda: exchange_t.wave(1)))
 
     def run_events(phase, at):
         for when, step, act in events:
@@ -375,18 +377,19 @@
             total = term if total is None else total + term
         return total
 
-    def away(start, size, number, step):
+    def away(start, size, number, k, step):
         to = col ^ step
         slot = lax.rem(number, 2)
-        src = ready.at[slot, :, pl.ds(to * plan.b_out, plan.b_out), pl.ds(0, size)]
-        dst = sums.at[step, :, :, pl.ds(start, size)]
+        src = ready.at[slot, k, pl.ds(to * plan.b_out, plan.b_out), pl.ds(0, size)]
+        dst = sums.at[step, k, :, pl.ds(start, size)]
+        at = number * plan.blocks + k
         if step == 0:
-            return pltpu.make_async_copy(src, dst, r_own.at[number])
+            return pltpu.make_async_copy(src, dst, r_own.at[at])
         return pltpu.make_async_remote_copy(
             src_ref=src,
             dst_ref=dst,
-            send_sem=r_send.at[number, step - 1],
-            recv_sem=r_recv.at[number, step - 1],
+            send_sem=r_send.at[at, step - 1],
+            recv_sem=r_recv.at[at, step - 1],
             device_id=(aa, to),
             device_id_type=MESH,
         )
@@ -401,24 +404,26 @@
         multiply(last, index)
 
     def left(start, size, number):
-        away(start, size, number, 0).wait()
-        for step in range(1, n_col):
-            away(start, size, number, step).wait_send()
-
-    def finish(start, size, number):
+        for k in range(plan.blocks):
+            away(start, size, number, k, 0).wait()
+            for step in range(1, n_col):
+                away(start, size, number, k, step).wait_send()
+
+    def finish(start, size, number, first=None):
         slot = lax.rem(number, 2)
 
         @pl.loop(0, plan.blocks)
         def _(k):
+            if first is not None:
+                pl.when(jnp.logical_and(number == 0, k == 1))(first)
             total = ladder(k, start, size)
             for at in range(0, plan.pairs, LANES):
                 made[0 : size * plan.b_size] = total[:, at : at + LANES]
                 for b in range(plan.b_size):
                     ready[slot, k, b, 0:size, at : at + LANES] = made[pl.ds(b, size, stride=plan.b_size), :]
-
-        for step in range(1, n_col):
-            away(start, size, number, step).start()
-        away(start, size, number, 0).start()
+            for step in range(1, n_col):
+                away(start, size, number, k, step).start()
+            away(start, size, number, k, 0).start()
 
     if last < 2:
         exchange_t.wave(0)
@@ -456,14 +461,15 @@
 
     t_begin(1, 0)
 
-    @pl.loop(0, inner)
-    def _(index):
-        @pl.when(index + 1 < inner)
-        def _():
-            t_begin(1, index + 1)
-
-        t_end(1, index)
-        t_work(1, index)
+    def t_second():
+        @pl.loop(0, inner)
+        def _(index):
+            @pl.when(index + 1 < inner)
+            def _():
+                t_begin(1, index + 1)
+
+            t_end(1, index)
+            t_work(1, index)
 
     bulk = plan.a_local // group - 1
 
@@ -479,7 +485,7 @@
         def _():
             left(pl.multiple_of((which - 2) * group, group), group, which - 2)
 
-        finish(pl.multiple_of(which * group, group), group, which)
+        finish(pl.multiple_of(which * group, group), group, which, t_second)
 
     tail, tail_inner = plan.tail, plan.tail // rows
     sent = [(which * group, group, jnp.int32(which)) for which in range(bulk)]
@@ -501,15 +507,16 @@
     for one in exchanges + [exchange_t]:
         one.finish()
     for start, size, number in sent:
-        for step in range(1, n_col):
-            away(start, size, number, step).wait_recv()
+        for k in range(plan.blocks):
+            for step in range(1, n_col):
+                away(start, size, number, k, step).wait_recv()
 
 
 def shards(n_aa, n_col, fit_ac, fit_bd, amplitudes):
     plan = Plan(n_aa, n_col, fit_ac, fit_bd, amplitudes)
     columns, count_q, c_local, pairs = plan.columns, plan.count_q, plan.c_local, plan.pairs
     dma, any_ = pltpu.SemaphoreType.DMA, pl.BlockSpec(memory_space=pl.ANY)
-    sends = plan.a_local // plan.group + 1
+    sends = (plan.a_local // plan.group + 1) * plan.blocks
     widths = [plan.depth * len(phase) for phase in plan.phases]
     most = max(len(phase) for phase in plan.phases)
     sums, _, _ = pl.pallas_call(

time: 161 us -> 147 us (0.913)
  Pallas kernels: 158 us -> 144 us
    pallas_call x1, Pallas kernels: 158 us -> 144 us  [shards(): pl.pallas_call(functools.partial(kernel, plan), in_specs=[any_] * 3, out_...]
where the time goes in v2:
time: 147 us; the launch traced here: 146 us
  Pallas kernels  144 us (98%)
  other arithmetic  2.59 us (2%)
    pallas_call x1, Pallas kernels, shards(): pl.pallas_call(functools.partial(kernel, plan), in_specs=[any_] * 3, out_...  144 us

profile of v2, /device:TPU:0, one launch (start us, length us, event | category | flops | bytes accessed | tf_op | source)
XLA Modules:
  0.0 146.5 jit_solution(863126192163132979)
XLA Ops:
  0.0 143.9 %shard_map.37 = (f32[4,2,4,64,256]{4,3,2,1,0:T(8,128)}, f32[2048,1024]{1,0:T(8,128)}, f32[2,32,128,256]{3,2,1,0:T(8,128)}) custom-call(f32[64,128,2048]{2,1,0:T(8,128)} %fit_ac.1, f32[64,1024]{1,0:T(8,128)} %fit_bd.1, f32[2,4,128,256]{3,2,1,0:T(8,128)} %amplitudes.1), custom_call_target="tpu_custom_call" | custom-call | tf_op jit(solution)/shard_map/pallas_call | solution.py:522
  143.9 2.6 %reduce_sum.9 = f32[2,4,64,256]{3,2,1,0:T(8,128)} reduce(f32[4,2,4,64,256]{4,3,2,1,0:T(8,128)} %get-tuple-element.6, f32[]{:T(128)} %constant.0.clone.1), dimensions={0}, to_apply=%region_0.0 | reduce | flops 393216 | bytes 2621444 | tf_op jit(solution)/shard_map/reduce_sum | solution.py:557
